TPU v7x, 32 devices: a whole 2x2x4 slice. The times are simulated.
32 devices in a mesh: groups: 2 (over x), expert: 2 (over core), tensor: 8 (over z, y).
Axes of the slice: x: 2, y: 2, z: 4, core: 2. Of those that a mesh axis runs over, the one named last changes fastest.
Arguments:
- tokens: bfloat16 [2048, 3072], P(('groups', 'expert', 'tensor')), parts along dimension 0, may hold values from -6 to 6
- expert_ids: int32 [2048, 1], P(('groups', 'expert', 'tensor')), parts along dimension 0, may hold values from 0 to 1; in each aligned block of 64 rows (0 to 63, 64 to 127, ...) at most 48 rows name the same one
- gates: float32 [2048], P(('groups', 'expert', 'tensor')), parts along dimension 0, may hold values from 0.2 to 1
- gate_weight: bfloat16 [2, 3072, 16384], P('expert', None, 'tensor'), may hold values from -0.109375 to 0.109375
- up_weight: bfloat16 [2, 3072, 16384], P('expert', None, 'tensor'), may hold values from -0.109375 to 0.109375
- down_weight: bfloat16 [2, 16384, 3072], P('expert', 'tensor'), may hold values from -0.046875 to 0.046875
Outputs:
- routed: bfloat16 [2048, 3072], P(('groups', 'expert', 'tensor')), parts along dimension 0
There are 2 independent parts, one for each index of `groups`. A program takes and returns all parts, laid end to end along the dimension named above; an argument that names none is the same for every part. Nothing has to cross between parts.
Inputs may be any that keep to these rules, and one draw needn't show every extreme that they name: `expert_ids`: among the 64 rows of one device no expert is named more than 48 times; in every draw some device names one expert exactly 48 times.
All inputs are finite; a program needn't handle non-finite values.
Results may differ from a plain program's by a relative error of at most 0.014.
Values may be sent and summed in bfloat16 or wider, within the bound.
A program may use at most 128 MiB of HBM per device.

v0:
```python
import jax
import jax.numpy as jnp
from jax import lax
from jax.sharding import PartitionSpec as P

CAP = 48
IN_CHUNKS = 1
OUT_CHUNKS = 2


def slot_table(expert_ids, experts):
    expert_of = expert_ids[:, 0]
    matches = (expert_of[:, None] == jnp.arange(experts, dtype=jnp.int32)[None, :]).astype(
        jnp.int32
    )
    earlier = jnp.cumsum(matches, axis=0) - matches
    position = jnp.sum(earlier * matches, axis=1)
    column = expert_of * CAP + position
    return (column[:, None] == jnp.arange(experts * CAP, dtype=jnp.int32)[None, :]).astype(
        jnp.bfloat16
    )


def per_device(tokens, expert_ids, gates, gate_weight, up_weight, down_weight):
    rows, width = tokens.shape
    experts = lax.axis_size("expert") * gate_weight.shape[0]
    tensor_size = lax.axis_size("tensor")
    group_ids = lax.all_gather(expert_ids, "tensor", axis=0, tiled=True)
    tables = jax.vmap(slot_table, in_axes=(0, None))(
        group_ids.reshape(tensor_size, rows, 1), experts
    )
    gate_pre, up_pre = (None, None)
    step = width // IN_CHUNKS
    for chunk in range(IN_CHUNKS):
        cut = slice(chunk * step, (chunk + 1) * step)
        gathered = lax.all_gather(tokens[:, cut], "tensor", axis=0)
        outgoing = jnp.einsum("trj,trd->tjd", tables, gathered, preferred_element_type=jnp.float32)
        outgoing = outgoing.astype(jnp.bfloat16).reshape(tensor_size, experts, CAP, step)
        arrived = lax.all_to_all(
            outgoing, "expert", split_axis=1, concat_axis=1, tiled=True
        ).reshape(tensor_size * experts * CAP, step)
        gate_part = jnp.dot(arrived, gate_weight[0, cut], preferred_element_type=jnp.float32)
        up_part = jnp.dot(arrived, up_weight[0, cut], preferred_element_type=jnp.float32)
        gate_pre = gate_part if gate_pre is None else gate_pre + gate_part
        up_pre = up_part if up_pre is None else up_pre + up_part
    hidden = (jax.nn.gelu(gate_pre, approximate=True) * up_pre).astype(jnp.bfloat16)
    step = width // OUT_CHUNKS
    pieces = []
    for chunk in range(OUT_CHUNKS):
        cut = slice(chunk * step, (chunk + 1) * step)
        product = jnp.dot(hidden, down_weight[0, :, cut], preferred_element_type=jnp.float32)
        product = product.astype(jnp.bfloat16).reshape(tensor_size, experts, CAP, step)
        returned = lax.all_to_all(
            product, "expert", split_axis=1, concat_axis=1, tiled=True
        ).reshape(tensor_size, experts * CAP, step)
        placed = jnp.einsum("trj,tjd->trd", tables, returned, preferred_element_type=jnp.float32)
        placed = placed.astype(jnp.bfloat16).reshape(tensor_size * rows, step)
        summed = lax.psum_scatter(placed, "tensor", scatter_dimension=0, tiled=True)
        pieces.append((summed.astype(jnp.float32) * gates[:, None]).astype(jnp.bfloat16))
    return jnp.concatenate(pieces, axis=1) if len(pieces) > 1 else pieces[0]


def solution(mesh):
    return jax.shard_map(
        per_device,
        mesh=mesh,
        in_specs=(
            P(("groups", "expert", "tensor"), None),
            P(("groups", "expert", "tensor"), None),
            P(("groups", "expert", "tensor")),
            P("expert", None, "tensor"),
            P("expert", None, "tensor"),
            P("expert", "tensor", None),
        ),
        out_specs=P(("groups", "expert", "tensor"), None),
        check_vma=False,
    )
```

profile of v0, /device:TPU:0, one launch (start us, length us, event | category | flops | bytes accessed | tf_op | source)
XLA Modules:
  0.0 267.2 jit_solution(1103878211246702654)
XLA Ops:
  6.5 0.0 all-gather.3.cloned.1.call-start
  6.5 0.7 all-gather.3.cloned.1.call-update
  7.3 0.0 reduce-scatter.5.cloned.1.call-start
  7.3 1.2 dynamic-slice
  9.2 0.8 bitcast_dynamic-update-slice_fusion
  10.0 13.1 %all-reduce = s32[512]{0:T(512)S(1)} all-reduce(s32[512]{0:T(512)S(1)} %bitcast_dynamic-update-slice_fusion), channel_id=1, replica_groups=mesh['groups'=2,'expert'=2,'tensor'=8] {'tensor'}, use_global_device_ids=true, to_apply=%add | all-reduce | flops 512 | bytes 4096
  23.1 0.1 squeeze_reshape.4
  23.1 0.1 copy.26
  23.2 1.4 fusion.33
  24.6 0.1 copy.27
  24.7 47.6 %all-gather.3.cloned.1.call-done = bf16[512,3072]{1,0:T(8,128)(2,1)} async-done(((bf16[64,3072]{1,0:T(8,128)(2,1)}), bf16[512,3072]{1,0:T(8,128)(2,1)}) %all-gather.3.cloned.1.call-update) | async-done | bytes 3145744 | tf_op jit(solution)/shard_map/all_gather | solution.py:36
  72.3 3.4 %convolution_convert_fusion = bf16[8,96,3072]{2,1,0:T(8,128)(2,1)S(1)} fusion(bf16[8,64,3072]{2,1,0:T(8,128)(2,1)} %bitcast.44, s32[8,64]{1,0:T(8,128)S(1)} %multiply_add_fusion), kind=kOutput, calls=%fused_computation.20 | convolution fusion | flops 304398336 | bytes 7866368 | tf_op jit(solution)/shard_map/trj,trd->tjd/dot_general | solution.py:37
  75.7 0.0 slice-start
  75.7 0.4 copy.28
  76.1 0.0 slice-start.1
  76.1 7.9 %all_to_all.15 = bf16[8,2,48,3072]{3,2,0,1:T(8,128)(2,1)S(1)} all-to-all(bf16[8,2,48,3072]{3,2,0,1:T(8,128)(2,1)S(1)} %copy.28), channel_id=1, replica_groups=mesh['groups'=2,'expert'=2,'tensor'=8] {'expert'}, dimensions={1} | all-to-all | bytes 9437184 | tf_op jit(solution)/shard_map/all_to_all | solution.py:39
  84.1 0.0 slice-start.2
  84.1 0.4 copy.29
  84.5 0.0 slice-done
  84.5 0.0 slice-done.1
  84.5 1.7 slice-done.2
  86.2 10.0 %fusion.2 = f32[768,2048]{1,0:T(8,128)S(1)} fusion(bf16[768,3072]{1,0:T(8,128)(2,1)S(1)} %bitcast.42, bf16[1,3072,2048]{2,1,0:T(8,128)(2,1)S(1)} %bitcast.48), kind=kOutput, calls=%fused_computation.2 | convolution fusion | flops 9663676416 | bytes 23592960 | tf_op jit(solution)/shard_map/dot_general | solution.py:42
  96.2 14.0 %fusion.12 = bf16[768,2048]{1,0:T(8,128)(2,1)S(1)} fusion(f32[768,2048]{1,0:T(8,128)S(1)} %fusion.2, bf16[768,3072]{1,0:T(8,128)(2,1)S(1)} %bitcast.43, bf16[1,3072,2048]{2,1,0:T(8,128)(2,1)} %param.10), kind=kOutput, calls=%fused_computation.13 | convolution fusion | flops 9679405056 | bytes 26738688 | tf_op jit(solution)/shard_map/dot_general | solution.py:43
  110.3 8.3 %fusion.24 = bf16[768,1536]{1,0:T(8,128)(2,1)S(1)} fusion(bf16[768,2048]{1,0:T(8,128)(2,1)S(1)} %fusion.12, bf16[1,2048,3072]{2,1,0:T(8,128)(2,1)} %param.11), kind=kOutput, calls=%fused_computation.22 | convolution fusion | flops 4833017856 | bytes 11796480 | tf_op jit(solution)/shard_map/dot_general | solution.py:51
  118.6 0.2 copy.32
  118.7 5.6 %all_to_all.16 = bf16[8,2,48,1536]{3,2,0,1:T(8,128)(2,1)S(1)} all-to-all(bf16[8,2,48,1536]{3,2,0,1:T(8,128)(2,1)S(1)} %copy.32), channel_id=1, replica_groups=mesh['groups'=2,'expert'=2,'tensor'=8] {'expert'}, dimensions={1} | all-to-all | bytes 4718592 | tf_op jit(solution)/shard_map/all_to_all | solution.py:53
  124.4 0.2 copy.33
  124.5 1.8 convolution_convert_fusion.1
  126.3 0.0 reduce-scatter.5.cloned.1.call-update
  126.4 0.0 reduce-scatter.3.cloned.1.call-start
  126.4 8.1 %fusion.21 = bf16[768,1536]{1,0:T(8,128)(2,1)S(1)} fusion(bf16[768,2048]{1,0:T(8,128)(2,1)S(1)} %fusion.12, bf16[1,2048,3072]{2,1,0:T(8,128)(2,1)} %param.11), kind=kOutput, calls=%fused_computation.21 | convolution fusion | flops 4833017856 | bytes 11796480 | tf_op jit(solution)/shard_map/dot_general | solution.py:51
  134.5 0.2 copy.30
  134.7 5.6 %all_to_all.17 = bf16[8,2,48,1536]{3,2,0,1:T(8,128)(2,1)S(1)} all-to-all(bf16[8,2,48,1536]{3,2,0,1:T(8,128)(2,1)S(1)} %copy.30), channel_id=1, replica_groups=mesh['groups'=2,'expert'=2,'tensor'=8] {'expert'}, dimensions={1} | all-to-all | bytes 4718592 | tf_op jit(solution)/shard_map/all_to_all | solution.py:53
  140.3 0.0 copy-start
  140.3 0.2 copy.31
  140.5 1.8 convolution_convert_fusion.2
  142.3 0.0 reduce-scatter.3.cloned.1.call-update
  142.3 48.5 %reduce-scatter.5.cloned.1.call-done = bf16[64,1536]{1,0:T(8,128)(2,1)} async-done(((bf16[512,1536]{1,0:T(8,128)(2,1)}), bf16[64,1536]{1,0:T(8,128)(2,1)}) %reduce-scatter.5.cloned.1.call-update) | async-done | bytes 196624 | tf_op jit(solution)/shard_map/reduce_scatter | solution.py:58
  190.8 67.9 %reduce-scatter.3.cloned.1.call-done = bf16[64,1536]{1,0:T(8,128)(2,1)} async-done(((bf16[512,1536]{1,0:T(8,128)(2,1)}), bf16[64,1536]{1,0:T(8,128)(2,1)}) %reduce-scatter.3.cloned.1.call-update) | async-done | bytes 196624 | tf_op jit(solution)/shard_map/reduce_scatter | solution.py:58
  258.7 0.0 copy-done
  258.7 1.2 multiply_convert_fusion.1
  259.9 0.8 pad_maximum_fusion
  (3 shorter events, 0.0 us)
Async XLA Ops:
  6.5 65.8 %all-gather.3.cloned.1.call-start = ((), (), s32[]{:S(2)}) async-start(), calls=%async_computation.7 | async-start | bytes 3538944 | tf_op jit(solution)/shard_map/all_gather | solution.py:36
  7.3 183.5 %reduce-scatter.5.cloned.1.call-start = ((), (), s32[]{:S(2)}) async-start(), calls=%async_computation.6 | async-start | bytes 1769472 | tf_op jit(solution)/shard_map/reduce_scatter | solution.py:58
  75.7 8.8 %slice-start = ((s8[12582912]{0:T(1024)(128)(4,1)}), s8[4194304]{0:T(1024)(128)(4,1)S(1)}, s32[]{:S(2)}) async-start(s8[12582912]{0:T(1024)(128)(4,1)} %bitcast.47), calls=%async_computation.8 | async-start | bytes 8388608
  76.1 8.4 %slice-start.1 = ((s8[12582912]{0:T(1024)(128)(4,1)}), s8[4194304]{0:T(1024)(128)(4,1)S(1)}, s32[]{:S(2)}) async-start(s8[12582912]{0:T(1024)(128)(4,1)} %bitcast.47), calls=%async_computation.9 | async-start | bytes 8388608
  84.1 2.2 slice-start.2
  126.4 132.3 %reduce-scatter.3.cloned.1.call-start = ((), (), s32[]{:S(2)}) async-start(), calls=%async_computation.5 | async-start | bytes 1769472 | tf_op jit(solution)/shard_map/reduce_scatter | solution.py:58
  140.3 118.4 %copy-start = (f32[64]{0:T(128)S(1)}, f32[64]{0:T(128)}, u32[]{:S(2)}) copy-start(f32[64]{0:T(128)} %param.8) | copy-start | bytes 772
Sparse Core Ops, SparseCore 0:
  9.5 62.7 all-gather.2
  126.5 64.2 reduce-scatter.4
  194.2 64.4 reduce-scatter.2
where the time goes:
time: 268 us; the launch traced here: 267 us
  waiting for transfers between devices  165 us (62%)
  matrix products  47.3 us (18%)
  blocking collectives  32.3 us (12%)
  between operations  13.9 us (5%)
  local copies, waits for them, and re-layouts  5.52 us (2%)
  other arithmetic  3.31 us (1%)
    reduce_scatter x2, waiting for transfers between devices, per_device(): summed = lax.psum_scatter(placed, 'tensor', scatter_dimension=0, tiled=True)  116 us
    all_gather x1, waiting for transfers between devices, per_device(): gathered = lax.all_gather(tokens[:, cut], 'tensor', axis=0)  47.6 us
    dot_general x2, matrix products, per_device(): jnp.dot(hidden, down_weight[0, :, cut], preferred_element_type=jnp.float32)  16.4 us
    dot_general x1, matrix products, per_device(): jnp.dot(arrived, up_weight[0, cut], preferred_element_type=jnp.float32)  14 us
    unnamed x1, blocking collectives  13.1 us
    all_to_all x2, blocking collectives, per_device(): lax.all_to_all(product, 'expert', split_axis=1, concat_axis=1, tiled=True)  11.3 us
    dot_general x1, matrix products, per_device(): jnp.dot(arrived, gate_weight[0, cut], preferred_element_type=jnp.float32)  9.97 us
    all_to_all x1, blocking collectives, per_device(): lax.all_to_all(outgoing, 'expert', split_axis=1, concat_axis=1, tiled=True)  7.92 us
  transfers between devices with their start and end apart: 3, of which 3 were waited for; matrix products, arithmetic and copies ran while one was open for 5% of the time, Pallas kernels for 0%

commit v1 on v0

--- a/solution.py
+++ b/solution.py
@@ -2,6 +2,7 @@
 import jax.numpy as jnp
 from jax import lax
 from jax.sharding import PartitionSpec as P
+from jax.lax import all_to_all, axis_size
 
 CAP = 48
 IN_CHUNKS = 1
@@ -50,8 +51,14 @@
         cut = slice(chunk * step, (chunk + 1) * step)
         product = jnp.dot(hidden, down_weight[0, :, cut], preferred_element_type=jnp.float32)
         product = product.astype(jnp.bfloat16).reshape(tensor_size, experts, CAP, step)
-        returned = lax.all_to_all(
-            product, "expert", split_axis=1, concat_axis=1, tiled=True
+        returned = jnp.concatenate(
+            all_to_all(
+                jnp.stack(jnp.split(product, axis_size("expert"), axis=1)),
+                "expert",
+                split_axis=0,
+                concat_axis=0,
+            ),
+            axis=1,
         ).reshape(tensor_size, experts * CAP, step)
         placed = jnp.einsum("trj,tjd->trd", tables, returned, preferred_element_type=jnp.float32)
         placed = placed.astype(jnp.bfloat16).reshape(tensor_size * rows, step)

time: 268 us -> 268 us (level)
  no operation moved by 1% of the time
where the time goes in v1:
time: 268 us; the launch traced here: 267 us
  waiting for transfers between devices  165 us (62%)
  matrix products  47.3 us (18%)
  blocking collectives  32.3 us (12%)
  between operations  13.9 us (5%)
  local copies, waits for them, and re-layouts  5.53 us (2%)
  other arithmetic  3.74 us (1%)
    reduce_scatter x2, waiting for transfers between devices, per_device(): summed = lax.psum_scatter(placed, 'tensor', scatter_dimension=0, tiled=True)  116 us
    all_gather x1, waiting for transfers between devices, per_device(): gathered = lax.all_gather(tokens[:, cut], 'tensor', axis=0)  47.6 us
    dot_general x2, matrix products, per_device(): jnp.dot(hidden, down_weight[0, :, cut], preferred_element_type=jnp.float32)  16.4 us
    dot_general x1, matrix products, per_device(): jnp.dot(arrived, up_weight[0, cut], preferred_element_type=jnp.float32)  14 us
    unnamed x1, blocking collectives  13.1 us
    all_to_all x2, blocking collectives, per_device(): all_to_all(jnp.stack(jnp.split(product, axis_size('expert'), axis=1)), 'e...  11.3 us
    dot_general x1, matrix products, per_device(): jnp.dot(arrived, gate_weight[0, cut], preferred_element_type=jnp.float32)  9.97 us
    all_to_all x1, blocking collectives, per_device(): lax.all_to_all(outgoing, 'expert', split_axis=1, concat_axis=1, tiled=True)  7.92 us
  transfers between devices with their start and end apart: 3, of which 3 were waited for; matrix products, arithmetic and copies ran while one was open for 5% of the time, Pallas kernels for 0%

profile of v1, /device:TPU:0, one launch (start us, length us, event | category | flops | bytes accessed | tf_op | source)
XLA Modules:
  0.0 267.4 jit_solution(1313389533321267239)
XLA Ops:
  6.5 0.0 all-gather.3.cloned.1.call-start
  6.5 0.7 all-gather.3.cloned.1.call-update
  7.3 0.0 reduce-scatter.3.cloned.1.call-start
  7.3 1.2 dynamic-slice
  9.2 0.8 bitcast_dynamic-update-slice_fusion
  10.0 13.1 %all-reduce = s32[512]{0:T(512)S(1)} all-reduce(s32[512]{0:T(512)S(1)} %bitcast_dynamic-update-slice_fusion), channel_id=1, replica_groups=mesh['groups'=2,'expert'=2,'tensor'=8] {'tensor'}, use_global_device_ids=true, to_apply=%add | all-reduce | flops 512 | bytes 4096
  23.1 0.1 squeeze_reshape.4
  23.1 0.1 copy.34
  23.2 1.4 fusion.33
  24.6 0.1 copy.35
  24.7 47.6 %all-gather.3.cloned.1.call-done = bf16[512,3072]{1,0:T(8,128)(2,1)} async-done(((bf16[64,3072]{1,0:T(8,128)(2,1)}), bf16[512,3072]{1,0:T(8,128)(2,1)}) %all-gather.3.cloned.1.call-update) | async-done | bytes 3145744 | tf_op jit(solution)/shard_map/all_gather | solution.py:37
  72.3 3.4 %convolution_convert_fusion = bf16[8,96,3072]{2,1,0:T(8,128)(2,1)S(1)} fusion(bf16[8,64,3072]{2,1,0:T(8,128)(2,1)} %bitcast.60, s32[8,64]{1,0:T(8,128)S(1)} %multiply_add_fusion), kind=kOutput, calls=%fused_computation.20 | convolution fusion | flops 304398336 | bytes 7866368 | tf_op jit(solution)/shard_map/trj,trd->tjd/dot_general | solution.py:38
  75.7 0.0 slice-start
  75.7 0.4 copy.36
  76.1 0.0 slice-start.1
  76.1 7.9 %all_to_all.15 = bf16[8,2,48,3072]{3,2,0,1:T(8,128)(2,1)S(1)} all-to-all(bf16[8,2,48,3072]{3,2,0,1:T(8,128)(2,1)S(1)} %copy.36), channel_id=1, replica_groups=mesh['groups'=2,'expert'=2,'tensor'=8] {'expert'}, dimensions={1} | all-to-all | bytes 9437184 | tf_op jit(solution)/shard_map/all_to_all | solution.py:40
  84.1 0.0 slice-start.2
  84.1 0.4 copy.37
  84.5 0.0 slice-done
  84.5 0.0 slice-done.1
  84.5 1.7 slice-done.2
  86.2 10.0 %fusion.2 = f32[768,2048]{1,0:T(8,128)S(1)} fusion(bf16[768,3072]{1,0:T(8,128)(2,1)S(1)} %bitcast.58, bf16[1,3072,2048]{2,1,0:T(8,128)(2,1)S(1)} %bitcast.64), kind=kOutput, calls=%fused_computation.2 | convolution fusion | flops 9663676416 | bytes 23592960 | tf_op jit(solution)/shard_map/dot_general | solution.py:43
  96.2 14.0 %fusion.12 = bf16[768,2048]{1,0:T(8,128)(2,1)S(1)} fusion(f32[768,2048]{1,0:T(8,128)S(1)} %fusion.2, bf16[768,3072]{1,0:T(8,128)(2,1)S(1)} %bitcast.59, bf16[1,3072,2048]{2,1,0:T(8,128)(2,1)} %param.10), kind=kOutput, calls=%fused_computation.13 | convolution fusion | flops 9679405056 | bytes 26738688 | tf_op jit(solution)/shard_map/dot_general | solution.py:44
  110.3 8.3 %fusion.21 = bf16[768,1536]{1,0:T(8,128)(2,1)S(1)} fusion(bf16[768,2048]{1,0:T(8,128)(2,1)S(1)} %fusion.12, bf16[1,2048,3072]{2,1,0:T(8,128)(2,1)} %param.11), kind=kOutput, calls=%fused_computation.21 | convolution fusion | flops 4833017856 | bytes 11796480 | tf_op jit(solution)/shard_map/dot_general | solution.py:52
  118.6 0.2 slice_bitcast_fusion.3
  118.7 0.2 pad_maximum_fusion
  119.0 5.6 %all_to_all.16 = bf16[2,8,1,48,1536]{4,3,1,2,0:T(8,128)(2,1)S(1)} all-to-all(bf16[2,8,1,48,1536]{4,3,1,2,0:T(8,128)(2,1)S(1)} %pad_maximum_fusion), channel_id=1, replica_groups=mesh['groups'=2,'expert'=2,'tensor'=8] {'expert'}, dimensions={0} | all-to-all | bytes 4718592 | tf_op jit(solution)/shard_map/all_to_all | solution.py:55
  124.6 0.2 copy.39
  124.8 1.8 convolution_convert_fusion.2
  126.6 0.0 reduce-scatter.3.cloned.1.call-update
  126.6 0.0 reduce-scatter.5.cloned.1.call-start
  126.6 8.1 %fusion.24 = bf16[768,1536]{1,0:T(8,128)(2,1)S(1)} fusion(bf16[768,2048]{1,0:T(8,128)(2,1)S(1)} %fusion.12, bf16[1,2048,3072]{2,1,0:T(8,128)(2,1)} %param.11), kind=kOutput, calls=%fused_computation.22 | convolution fusion | flops 4833017856 | bytes 11796480 | tf_op jit(solution)/shard_map/dot_general | solution.py:52
  134.7 0.2 slice_bitcast_fusion.1
  134.9 0.2 pad_maximum_fusion.1
  135.1 5.6 %all_to_all.17 = bf16[2,8,1,48,1536]{4,3,1,2,0:T(8,128)(2,1)S(1)} all-to-all(bf16[2,8,1,48,1536]{4,3,1,2,0:T(8,128)(2,1)S(1)} %pad_maximum_fusion.1), channel_id=1, replica_groups=mesh['groups'=2,'expert'=2,'tensor'=8] {'expert'}, dimensions={0} | all-to-all | bytes 4718592 | tf_op jit(solution)/shard_map/all_to_all | solution.py:55
  140.7 0.2 copy.41
  140.9 0.0 copy-start
  140.9 1.8 convolution_convert_fusion.1
  142.7 0.0 reduce-scatter.5.cloned.1.call-update
  142.7 48.2 %reduce-scatter.3.cloned.1.call-done = bf16[64,1536]{1,0:T(8,128)(2,1)} async-done(((bf16[512,1536]{1,0:T(8,128)(2,1)}), bf16[64,1536]{1,0:T(8,128)(2,1)}) %reduce-scatter.3.cloned.1.call-update) | async-done | bytes 196624 | tf_op jit(solution)/shard_map/reduce_scatter | solution.py:65
  191.0 68.0 %reduce-scatter.5.cloned.1.call-done = bf16[64,1536]{1,0:T(8,128)(2,1)} async-done(((bf16[512,1536]{1,0:T(8,128)(2,1)}), bf16[64,1536]{1,0:T(8,128)(2,1)}) %reduce-scatter.5.cloned.1.call-update) | async-done | bytes 196624 | tf_op jit(solution)/shard_map/reduce_scatter | solution.py:65
  258.9 0.0 copy-done
  258.9 1.2 multiply_convert_fusion.1
  260.1 0.8 pad_maximum_fusion.2
  (3 shorter events, 0.0 us)
Async XLA Ops:
  6.5 65.8 %all-gather.3.cloned.1.call-start = ((), (), s32[]{:S(2)}) async-start(), calls=%async_computation.7 | async-start | bytes 3538944 | tf_op jit(solution)/shard_map/all_gather | solution.py:37
  7.3 183.7 %reduce-scatter.3.cloned.1.call-start = ((), (), s32[]{:S(2)}) async-start(), calls=%async_computation.5 | async-start | bytes 1769472 | tf_op jit(solution)/shard_map/reduce_scatter | solution.py:65
  75.7 8.8 %slice-start = ((s8[12582912]{0:T(1024)(128)(4,1)}), s8[4194304]{0:T(1024)(128)(4,1)S(1)}, s32[]{:S(2)}) async-start(s8[12582912]{0:T(1024)(128)(4,1)} %bitcast.63), calls=%async_computation.8 | async-start | bytes 8388608
  76.1 8.4 %slice-start.1 = ((s8[12582912]{0:T(1024)(128)(4,1)}), s8[4194304]{0:T(1024)(128)(4,1)S(1)}, s32[]{:S(2)}) async-start(s8[12582912]{0:T(1024)(128)(4,1)} %bitcast.63), calls=%async_computation.9 | async-start | bytes 8388608
  84.1 2.2 slice-start.2
  126.6 132.4 %reduce-scatter.5.cloned.1.call-start = ((), (), s32[]{:S(2)}) async-start(), calls=%async_computation.6 | async-start | bytes 1769472 | tf_op jit(solution)/shard_map/reduce_scatter | solution.py:65
  140.9 118.0 %copy-start = (f32[64]{0:T(128)S(1)}, f32[64]{0:T(128)}, u32[]{:S(2)}) copy-start(f32[64]{0:T(128)} %param.8) | copy-start | bytes 772
Sparse Core Ops, SparseCore 0:
  9.5 62.7 all-gather.2
  126.7 64.2 reduce-scatter.2
  194.4 64.4 reduce-scatter.4
